TPU v7x, 32 devices: a whole 2x2x4 slice. The times are simulated.
32 devices in a mesh: fsdp: 16 (over z, y, x), tp: 2 (over core).
Axes of the slice: x: 2, y: 2, z: 4, core: 2. Of those that a mesh axis runs over, the one named last changes fastest.
Arguments:
- tokens: bfloat16 [2, 2048, 8192], P(None, 'fsdp', 'tp'), may hold values from -6 to 6
- frozen_weight: bfloat16 [8192, 2048], P('tp', 'fsdp'), may hold values from -0.0625 to 0.0625
- cotangent: bfloat16 [2, 2048, 2048], P(None, 'fsdp'), may hold values from -6 to 6
- block_adapter_index: int32 [2, 16], replicated, may hold values from 0 to 511
- down_weight: bfloat16 [512, 8192, 16], P(None, ('tp', 'fsdp')), may hold values from -0.0625 to 0.0625
- up_weight: bfloat16 [512, 16, 2048], P(None, None, ('tp', 'fsdp')), may hold values from -0.125 to 0.125
Outputs:
- key_value_output: bfloat16 [2, 2048, 2048], P(None, 'fsdp', 'tp')
- input_gradient: bfloat16 [2, 2048, 8192], P(None, 'fsdp', 'tp')
- grad_down: float32 [512, 8192, 16], P(None, ('tp', 'fsdp'))
- up_weight_gradient: float32 [512, 16, 2048], P(None, None, ('tp', 'fsdp'))
Inputs may be any that keep to these rules, and one draw needn't show every extreme that they name: `block_adapter_index`: one adapter for each block of 128 rows of a microbatch.
All inputs are finite; a program needn't handle non-finite values.
Results may differ from a plain program's by a relative error of at most 0.005.
Values may be sent and summed in bfloat16 or wider, within the bound.
No kernel may reach another device: no remote copies, remote signals or barrier semaphores. Data moves between devices by JAX's collectives and lax.ppermute only.
A program may use at most 128 MiB of HBM per device.

v0:
```python
import jax
import jax.numpy as jnp
from jax import lax
from jax.sharding import PartitionSpec as P

BLOCK = 128
adapter_scale = 2.0


def selected_sum(adapter_selector, tiles):
    flat = tiles.reshape(tiles.shape[0], -1)
    return lax.dot_general(
        adapter_selector,
        flat,
        (((0,), (0,)), ((), ())),
        precision=lax.Precision.HIGHEST,
        preferred_element_type=jnp.float32,
    )


def local(tokens, frozen_weight, cotangent, block_adapter_index, down_weight, up_weight):
    microbatch_list, token_block_rows, shard_width = tokens.shape
    kv_width = cotangent.shape[2]
    key_value_slice = kv_width // lax.axis_size("tp")
    row_total = microbatch_list * token_block_rows
    tok_matrix = tokens.reshape(row_total, shard_width)
    cot_matrix = cotangent.reshape(row_total, kv_width)
    adapter_number = down_weight.shape[0]
    rank_width = down_weight.shape[2]
    adapter_range = jnp.arange(adapter_number, dtype=jnp.int32)
    gathered = lax.all_gather(frozen_weight, "fsdp", axis=1, tiled=True)
    kv_partial = jnp.dot(tok_matrix, gathered, preferred_element_type=jnp.float32)
    frozen_key_value = lax.psum_scatter(kv_partial, "tp", scatter_dimension=1, tiled=True)
    frozen_input_gradient = lax.dot_general(
        cot_matrix, gathered, (((1,), (1,)), ((), ())), preferred_element_type=jnp.float32
    )
    cot_slab = lax.dynamic_slice_in_dim(
        cotangent, lax.axis_index("tp") * key_value_slice, key_value_slice, 2
    )
    fsdp_count = lax.axis_size("fsdp")
    per_dev = token_block_rows // BLOCK
    dest_ids = (
        block_adapter_index.reshape(microbatch_list, fsdp_count, per_dev)
        .transpose(1, 0, 2)
        .reshape(fsdp_count, microbatch_list * per_dev)
    )
    down_send = jnp.take(down_weight, dest_ids, axis=0).transpose(0, 1, 3, 2)
    up_send = jnp.take(up_weight, dest_ids, axis=0)
    down_mine, up_mine = (
        lax.all_to_all(down_send, "fsdp", split_axis=0, concat_axis=3, tiled=True),
        lax.all_to_all(up_send, "fsdp", split_axis=0, concat_axis=3, tiled=True),
    )
    down_mine = down_mine.reshape(microbatch_list, per_dev, rank_width, shard_width)
    up_mine = up_mine.reshape(microbatch_list, per_dev, rank_width, key_value_slice)
    tok_blocks = tokens.reshape(microbatch_list, per_dev, BLOCK, shard_width)
    gradient_blocks = cot_slab.reshape(microbatch_list, per_dev, BLOCK, key_value_slice)
    low_part = jnp.einsum(
        "mnbc,mnrc->mnbr", tok_blocks, down_mine, preferred_element_type=jnp.float32
    )
    partial_input_gradient = adapter_scale * jnp.einsum(
        "fsvj,fsyj->fsvy", gradient_blocks, up_mine, preferred_element_type=jnp.float32
    )
    low_sum, back_sum = lax.psum((low_part, partial_input_gradient), "tp")
    low_rank = low_sum.astype(jnp.bfloat16)
    rank_gradient = back_sum.astype(jnp.bfloat16)
    adapter_key_value = (
        adapter_scale
        * jnp.einsum("elui,elis->elus", low_rank, up_mine, preferred_element_type=jnp.float32)
    ).astype(jnp.bfloat16)
    adapter_input_gradient = jnp.einsum(
        "mnbr,mnrc->mnbc", rank_gradient, down_mine, preferred_element_type=jnp.float32
    ).astype(jnp.bfloat16)
    adapter_key_value = adapter_key_value.reshape(
        microbatch_list, token_block_rows, key_value_slice
    )
    adapter_input_gradient = adapter_input_gradient.reshape(
        microbatch_list, token_block_rows, shard_width
    )
    down_tiles = jnp.einsum(
        "mnbc,mnbr->mnrc", tok_blocks, rank_gradient, preferred_element_type=jnp.float32
    )
    up_weight_tiles = adapter_scale * jnp.einsum(
        "puai,puac->puic", low_rank, gradient_blocks, preferred_element_type=jnp.float32
    )
    down_tiles = down_tiles.reshape(microbatch_list * per_dev, rank_width, shard_width)
    up_weight_tiles = up_weight_tiles.reshape(
        microbatch_list * per_dev, rank_width, key_value_slice
    )
    down_owned, up_owned = (
        lax.all_to_all(
            down_tiles.astype(jnp.bfloat16), "fsdp", split_axis=2, concat_axis=0, tiled=True
        ).astype(down_tiles.dtype),
        lax.all_to_all(
            up_weight_tiles.astype(jnp.bfloat16), "fsdp", split_axis=2, concat_axis=0, tiled=True
        ).astype(up_weight_tiles.dtype),
    )
    owned_ids = dest_ids.reshape(-1)
    adapter_selector = (owned_ids[:, None] == adapter_range[None, :]).astype(jnp.float32)
    grad_down = (
        selected_sum(adapter_selector, down_owned)
        .reshape(adapter_number, rank_width, down_weight.shape[1])
        .transpose(0, 2, 1)
    )
    up_weight_gradient = selected_sum(adapter_selector, up_owned).reshape(up_weight.shape)
    key_value_output = (
        frozen_key_value.reshape(microbatch_list, token_block_rows, key_value_slice)
        + adapter_key_value.astype(jnp.float32)
    ).astype(jnp.bfloat16)
    input_gradient = (
        frozen_input_gradient.reshape(microbatch_list, token_block_rows, shard_width)
        + adapter_input_gradient.astype(jnp.float32)
    ).astype(jnp.bfloat16)
    return (key_value_output, input_gradient, grad_down, up_weight_gradient)


def solution(mesh):
    return jax.shard_map(
        local,
        mesh=mesh,
        in_specs=(
            P(None, "fsdp", "tp"),
            P("tp", "fsdp"),
            P(None, "fsdp", None),
            P(),
            P(None, ("tp", "fsdp"), None),
            P(None, None, ("tp", "fsdp")),
        ),
        out_specs=(
            P(None, "fsdp", "tp"),
            P(None, "fsdp", "tp"),
            P(None, ("tp", "fsdp"), None),
            P(None, None, ("tp", "fsdp")),
        ),
        check_vma=False,
    )
```

profile of v0, /device:TPU:0, one launch (start us, length us, event | category | flops | bytes accessed | tf_op | source)
XLA Modules:
  0.0 380.9 jit_solution(13523982944340229810)
XLA Ops:
  7.2 0.7 all-gather.2.cloned.1.call-update
  8.0 3.8 copy.30
  12.1 2.2 gather_fusion.1
  14.3 248.3 %all-gather.2.cloned.1.call-done = bf16[4096,2048]{1,0:T(8,128)(2,1)} async-done(((bf16[4096,128]{1,0:T(8,128)(2,1)}), bf16[4096,2048]{1,0:T(8,128)(2,1)}) %all-gather.2.cloned.1.call-update) | async-done | bytes 16777232 | tf_op jit(solution)/shard_map/all_gather | solution.py:31
  262.6 9.5 %fusion.36 = f32[256,2048]{1,0:T(8,128)} fusion(bf16[256,4096]{1,0:T(8,128)(2,1)S(1)} %bitcast.91, bf16[4096,2048]{1,0:T(8,128)(2,1)} %all-gather.2.cloned.1.call-done), kind=kOutput, calls=%fused_computation.46 | convolution fusion | flops 4294967296 | bytes 20971520 | tf_op jit(solution)/shard_map/dot_general | solution.py:32
  272.2 0.8 reshape.121
  272.9 3.8 all-to-all-start.1
  276.7 2.9 gather_fusion
  279.7 0.8 select_bitcast_fusion
  280.5 3.8 all-to-all-done.1
  284.3 3.5 all-to-all-start
  288.5 1.0 reshape.122
  289.5 0.7 copy.31
  290.2 1.0 reshape.97
  291.5 5.3 %all-to-all-done = bf16[16,2,16,256]{3,2,1,0:T(8,128)(2,1)S(1)} async-done(((bf16[16,2,16,256]{3,2,1,0:T(8,128)(2,1)}), bf16[16,2,16,256]{3,2,1,0:T(8,128)(2,1)S(1)}, u32[]{:S(2)}, u32[]{:S(2)}) %all-to-all-start) | async-done | bytes 262176 | tf_op jit(solution)/shard_map/all_to_all | solution.py:50
  296.8 0.9 copy.28
  297.7 1.1 reshape.95
  299.4 3.4 all-reduce
  303.4 1.2 reshape.125
  304.6 3.5 all-to-all-start.3
  308.5 3.8 copy.33
  312.3 7.3 %reshape.123 = bf16[16,2,4096]{2,1,0:T(2,128)(2,1)} reshape(bf16[4096,2,16]{2,1,0:T(2,128)(2,1)} %bitcast.93) | data formatting | bytes 524288
  319.7 6.9 %all-to-all-start.2 = ((bf16[16,2,4096]{2,1,0:T(2,128)(2,1)}), bf16[16,2,4096]{2,1,0:T(2,128)(2,1)S(1)}, u32[]{:S(2)}, u32[]{:S(2)}) async-start(bf16[16,2,4096]{2,1,0:T(2,128)(2,1)} %reshape.123), calls=%async_computation.3 | async-start | bytes 524288 | tf_op jit(solution)/shard_map/all_to_all | solution.py:90
  326.6 2.7 fusion.5
  330.3 1.8 fusion.19
  332.2 4.5 %all-to-all-done.2 = bf16[16,2,4096]{2,1,0:T(2,128)(2,1)S(1)} async-done(((bf16[16,2,4096]{2,1,0:T(2,128)(2,1)}), bf16[16,2,4096]{2,1,0:T(2,128)(2,1)S(1)}, u32[]{:S(2)}, u32[]{:S(2)}) %all-to-all-start.2) | async-done | bytes 262176 | tf_op jit(solution)/shard_map/all_to_all | solution.py:90
  336.6 2.4 reshape.124
  339.0 4.4 %copy.34 = bf16[2,16,16,256]{3,1,0,2:T(8,128)(2,1)S(1)} copy(bf16[2,16,16,256]{1,0,3,2:T(2,128)(2,1)} %bitcast.94) | data formatting | bytes 524288 | tf_op jit(solution)/shard_map/all_to_all | solution.py:90
  343.4 1.4 convolution_bitcast_fusion
  344.8 8.3 %copy.39 = f32[512,256,16]{1,2,0:T(8,128)} copy(f32[512,256,16]{1,0,2:T(8,128)S(1)} %convolution_bitcast_fusion) | data formatting | bytes 16777216
  353.1 18.7 %fusion.6 = bf16[2,128,4096]{2,1,0:T(8,128)(2,1)} fusion(f32[2,128,4096]{2,1,0:T(8,128)} %fusion.5, bf16[2,128,2048]{2,1,0:T(8,128)(2,1)S(1)} %copy-done.2, bf16[4096,2048]{1,0:T(8,128)(2,1)} %all-gather.2.cloned.1.call-done), kind=kOutput, calls=%fused_computation.7 | convolution fusion | flops 4297064448 | bytes 24117248 | tf_op jit(solution)/shard_map/dot_general | solution.py:34
  371.7 2.4 fusion.12
  (35 shorter events, 4.0 us)
Async XLA Ops:
  7.2 255.4 %copy-start = (bf16[2,128,4096]{2,1,0:T(8,128)(2,1)S(1)}, bf16[2,128,4096]{2,1,0:T(8,128)(2,1)}, u32[]{:S(2)}) copy-start(bf16[2,128,4096]{2,1,0:T(8,128)(2,1)} %param.6) | copy-start | bytes 6291460
  7.2 4.6 %copy-start.5 = (s32[2,16]{1,0:T(2,128)S(1)}, s32[2,16]{1,0:T(2,128)}, u32[]{:S(2)}) copy-start(s32[2,16]{1,0:T(2,128)} %param.9) | copy-start | bytes 388
  7.2 255.4 %all-gather.2.cloned.1.call-start = ((), (), s32[]{:S(2)}) async-start(), calls=%async_computation.5 | async-start | bytes 17825792 | tf_op jit(solution)/shard_map/all_gather | solution.py:31
  7.9 363.8 %reduce-scatter.2.cloned.1.call-start = ((), (), s32[]{:S(2)}) async-start(), calls=%async_computation.6 | async-start | bytes 3145728 | tf_op jit(solution)/shard_map/reduce_scatter | solution.py:33
  272.9 11.3 %all-to-all-start.1 = ((bf16[16,2,1024]{2,1,0:T(2,128)(2,1)}), bf16[16,2,1024]{2,1,0:T(2,128)(2,1)S(1)}, u32[]{:S(2)}, u32[]{:S(2)}) async-start(bf16[16,2,1024]{2,1,0:T(2,128)(2,1)} %reshape.121), calls=%async_computation.2 | async-start | bytes 131072 | tf_op jit(solution)/shard_map/all_to_all | solution.py:51
  276.7 14.5 %copy-start.1 = (bf16[2,128,2048]{2,1,0:T(8,128)(2,1)S(1)}, bf16[2,128,2048]{2,1,0:T(8,128)(2,1)}, u32[]{:S(2)}) copy-start(bf16[2,128,2048]{2,1,0:T(8,128)(2,1)} %param.8) | copy-start | bytes 3145732
  284.3 4.2 %copy-start.3 = (bf16[16,2,1024]{2,1,0:T(2,128)(2,1)}, bf16[16,2,1024]{2,1,0:T(2,128)(2,1)S(1)}, u32[]{:S(2)}) copy-start(bf16[16,2,1024]{2,1,0:T(2,128)(2,1)S(1)} %all-to-all-done.1) | copy-start | bytes 196612
  284.3 12.6 %all-to-all-start = ((bf16[16,2,16,256]{3,2,1,0:T(8,128)(2,1)}), bf16[16,2,16,256]{3,2,1,0:T(8,128)(2,1)S(1)}, u32[]{:S(2)}, u32[]{:S(2)}) async-start(bf16[16,2,16,256]{3,2,1,0:T(8,128)(2,1)} %select_bitcast_fusion), calls=%async_computation.1 | async-start | bytes 524288 | tf_op jit(solution)/shard_map/all_to_all | solution.py:50
  304.6 15.1 %all-to-all-start.3 = ((bf16[16,2,1024]{2,1,0:T(2,128)(2,1)}), bf16[16,2,1024]{2,1,0:T(2,128)(2,1)S(1)}, u32[]{:S(2)}, u32[]{:S(2)}) async-start(bf16[16,2,1024]{2,1,0:T(2,128)(2,1)} %reshape.125), calls=%async_computation.4 | async-start | bytes 131072 | tf_op jit(solution)/shard_map/all_to_all | solution.py:93
  319.7 16.9 %all-to-all-start.2 = ((bf16[16,2,4096]{2,1,0:T(2,128)(2,1)}), bf16[16,2,4096]{2,1,0:T(2,128)(2,1)S(1)}, u32[]{:S(2)}, u32[]{:S(2)}) async-start(bf16[16,2,4096]{2,1,0:T(2,128)(2,1)} %reshape.123), calls=%async_computation.3 | async-start | bytes 524288 | tf_op jit(solution)/shard_map/all_to_all | solution.py:90
  326.6 3.7 copy-start.4
  344.8 8.3 %copy-start.2 = (bf16[2,128,2048]{2,1,0:T(8,128)(2,1)S(1)}, bf16[2,128,2048]{2,1,0:T(8,128)(2,1)}, u32[]{:S(2)}) copy-start(bf16[2,128,2048]{2,1,0:T(8,128)(2,1)} %param.8) | copy-start | bytes 3145732
Sparse Core Ops, SparseCore 0:
  10.7 251.8 all-gather.1
  272.2 7.8 reduce-scatter.1
where the time goes:
time: 382 us; the launch traced here: 381 us
  waiting for transfers between devices  263 us (69%)
  local copies, waits for them, and re-layouts  44.1 us (12%)
  matrix products  37.8 us (10%)
  starting transfers between devices  17.9 us (5%)
  between operations  14.2 us (4%)
    all_gather x1, waiting for transfers between devices, local(): gathered = lax.all_gather(frozen_weight, 'fsdp', axis=1, tiled=True)  248 us
    unnamed x20, local copies, waits for them, and re-layouts  25.1 us
    dot_general x1, matrix products, local(): lax.dot_general(cot_matrix, gathered, (((1,), (1,)), ((), ())), preferred...  18.7 us
    dot_general x1, matrix products, local(): jnp.dot(tok_matrix, gathered, preferred_element_type=jnp.float32)  9.45 us
  transfers between devices with their start and end apart: 6, of which 4 were waited for; matrix products, arithmetic and copies ran while one was open for 19% of the time, Pallas kernels for 0%

commit v1 on v0

--- a/solution.py
+++ b/solution.py
@@ -28,7 +28,12 @@
     adapter_number = down_weight.shape[0]
     rank_width = down_weight.shape[2]
     adapter_range = jnp.arange(adapter_number, dtype=jnp.int32)
-    gathered = lax.all_gather(frozen_weight, "fsdp", axis=1, tiled=True)
+    ring = [frozen_weight]
+    for hop in range(15):
+        ring.append(lax.ppermute(ring[-1], "fsdp", [(dev, (dev + 1) % 16) for dev in range(16)]))
+    gathered = jnp.roll(
+        jnp.concatenate(ring[::-1], axis=1), (lax.axis_index("fsdp") + 1) * ring[0].shape[1], axis=1
+    )
     kv_partial = jnp.dot(tok_matrix, gathered, preferred_element_type=jnp.float32)
     frozen_key_value = lax.psum_scatter(kv_partial, "tp", scatter_dimension=1, tiled=True)
     frozen_input_gradient = lax.dot_general(

time: 382 us -> 539 us (1.41)
  waiting for transfers between devices: 263 us -> 345 us
  local copies, waits for them, and re-layouts: 44.1 us -> 111 us
  starting transfers between devices: 17.9 us -> 30.8 us
  matrix products: 37.8 us -> 28.9 us
    ppermute x0 -> x15, waiting for transfers between devices: none -> 341 us  [local(): lax.ppermute(ring[-1], 'fsdp', [(dev, (dev + 1) % 16) for dev in range(16)])]
    all_gather x1 -> x0, waiting for transfers between devices: 248 us -> none  [local(): gathered = lax.all_gather(frozen_weight, 'fsdp', axis=1, tiled=True)]
    unnamed x20 -> x99, local copies, waits for them, and re-layouts: 25.1 us -> 93.3 us
    dot_general x1, matrix products: 18.7 us -> 8.45 us  [local(): lax.dot_general(cot_matrix, gathered, (((1,), (1,)), ((), ())), preferred...]
  transfers between devices with their start and end apart: 6 -> 20, of which waited for: 4 -> 15; matrix products, arithmetic and copies ran while one was open for 19% -> 24% of each run, Pallas kernels for 0% -> 0%
where the time goes in v1:
time: 539 us; the launch traced here: 538 us
  waiting for transfers between devices  345 us (64%)
  local copies, waits for them, and re-layouts  111 us (21%)
  starting transfers between devices  30.8 us (6%)
  matrix products  28.9 us (5%)
  between operations  14.4 us (3%)
    ppermute x15, waiting for transfers between devices, local(): lax.ppermute(ring[-1], 'fsdp', [(dev, (dev + 1) % 16) for dev in range(16)])  341 us
    unnamed x99, local copies, waits for them, and re-layouts  93.3 us
  transfers between devices with their start and end apart: 20, of which 15 were waited for; matrix products, arithmetic and copies ran while one was open for 24% of the time, Pallas kernels for 0%

profile of v1, /device:TPU:0, one launch (start us, length us, event | category | flops | bytes accessed | tf_op | source)
XLA Modules:
  0.0 537.7 jit_solution(7147304414484572414)
XLA Ops:
  7.2 3.0 collective-permute-start
  10.2 27.4 %collective-permute-done = bf16[4096,128]{1,0:T(8,128)(2,1)S(1)} collective-permute-done((bf16[4096,128]{1,0:T(8,128)(2,1)}, bf16[4096,128]{1,0:T(8,128)(2,1)S(1)}, u32[]{:S(2)}, u32[]{:S(2)}) %collective-permute-start) | collective-permute-done | bytes 1048608 | tf_op jit(solution)/shard_map/ppermute | solution.py:33
  38.6 27.9 %collective-permute-done.1 = bf16[4096,128]{1,0:T(8,128)(2,1)S(1)} collective-permute-done((bf16[4096,128]{1,0:T(8,128)(2,1)S(1)}, bf16[4096,128]{1,0:T(8,128)(2,1)S(1)}, u32[]{:S(2)}, u32[]{:S(2)}) %collective-permute-start.1) | collective-permute-done | bytes 1048608 | tf_op jit(solution)/shard_map/ppermute | solution.py:33
  67.4 27.1 %collective-permute-done.2 = bf16[4096,128]{1,0:T(8,128)(2,1)S(1)} collective-permute-done((bf16[4096,128]{1,0:T(8,128)(2,1)S(1)}, bf16[4096,128]{1,0:T(8,128)(2,1)S(1)}, u32[]{:S(2)}, u32[]{:S(2)}) %collective-permute-start.2) | collective-permute-done | bytes 1048608 | tf_op jit(solution)/shard_map/ppermute | solution.py:33
  95.5 26.2 %collective-permute-done.3 = bf16[4096,128]{1,0:T(8,128)(2,1)S(1)} collective-permute-done((bf16[4096,128]{1,0:T(8,128)(2,1)S(1)}, bf16[4096,128]{1,0:T(8,128)(2,1)S(1)}, u32[]{:S(2)}, u32[]{:S(2)}) %collective-permute-start.3) | collective-permute-done | bytes 1048608 | tf_op jit(solution)/shard_map/ppermute | solution.py:33
  122.7 25.3 %collective-permute-done.4 = bf16[4096,128]{1,0:T(8,128)(2,1)S(1)} collective-permute-done((bf16[4096,128]{1,0:T(8,128)(2,1)S(1)}, bf16[4096,128]{1,0:T(8,128)(2,1)S(1)}, u32[]{:S(2)}, u32[]{:S(2)}) %collective-permute-start.4) | collective-permute-done | bytes 1048608 | tf_op jit(solution)/shard_map/ppermute | solution.py:33
  149.0 24.5 %collective-permute-done.5 = bf16[4096,128]{1,0:T(8,128)(2,1)S(1)} collective-permute-done((bf16[4096,128]{1,0:T(8,128)(2,1)S(1)}, bf16[4096,128]{1,0:T(8,128)(2,1)S(1)}, u32[]{:S(2)}, u32[]{:S(2)}) %collective-permute-start.5) | collective-permute-done | bytes 1048608 | tf_op jit(solution)/shard_map/ppermute | solution.py:33
  174.5 23.6 %collective-permute-done.6 = bf16[4096,128]{1,0:T(8,128)(2,1)S(1)} collective-permute-done((bf16[4096,128]{1,0:T(8,128)(2,1)S(1)}, bf16[4096,128]{1,0:T(8,128)(2,1)S(1)}, u32[]{:S(2)}, u32[]{:S(2)}) %collective-permute-start.6) | collective-permute-done | bytes 1048608 | tf_op jit(solution)/shard_map/ppermute | solution.py:33
  199.1 22.8 %collective-permute-done.7 = bf16[4096,128]{1,0:T(8,128)(2,1)S(1)} collective-permute-done((bf16[4096,128]{1,0:T(8,128)(2,1)S(1)}, bf16[4096,128]{1,0:T(8,128)(2,1)S(1)}, u32[]{:S(2)}, u32[]{:S(2)}) %collective-permute-start.7) | collective-permute-done | bytes 1048608 | tf_op jit(solution)/shard_map/ppermute | solution.py:33
  222.9 22.3 %collective-permute-done.8 = bf16[4096,128]{1,0:T(8,128)(2,1)S(1)} collective-permute-done((bf16[4096,128]{1,0:T(8,128)(2,1)S(1)}, bf16[4096,128]{1,0:T(8,128)(2,1)S(1)}, u32[]{:S(2)}, u32[]{:S(2)}) %collective-permute-start.8) | collective-permute-done | bytes 1048608 | tf_op jit(solution)/shard_map/ppermute | solution.py:33
  246.2 22.3 %collective-permute-done.9 = bf16[4096,128]{1,0:T(8,128)(2,1)S(1)} collective-permute-done((bf16[4096,128]{1,0:T(8,128)(2,1)S(1)}, bf16[4096,128]{1,0:T(8,128)(2,1)S(1)}, u32[]{:S(2)}, u32[]{:S(2)}) %collective-permute-start.9) | collective-permute-done | bytes 1048608 | tf_op jit(solution)/shard_map/ppermute | solution.py:33
  269.6 22.3 %collective-permute-done.10 = bf16[4096,128]{1,0:T(8,128)(2,1)S(1)} collective-permute-done((bf16[4096,128]{1,0:T(8,128)(2,1)S(1)}, bf16[4096,128]{1,0:T(8,128)(2,1)S(1)}, u32[]{:S(2)}, u32[]{:S(2)}) %collective-permute-start.10) | collective-permute-done | bytes 1048608 | tf_op jit(solution)/shard_map/ppermute | solution.py:33
  292.9 22.4 %collective-permute-done.11 = bf16[4096,128]{1,0:T(8,128)(2,1)S(1)} collective-permute-done((bf16[4096,128]{1,0:T(8,128)(2,1)S(1)}, bf16[4096,128]{1,0:T(8,128)(2,1)S(1)}, u32[]{:S(2)}, u32[]{:S(2)}) %collective-permute-start.11) | collective-permute-done | bytes 1048608 | tf_op jit(solution)/shard_map/ppermute | solution.py:33
  316.2 22.3 %collective-permute-done.12 = bf16[4096,128]{1,0:T(8,128)(2,1)S(1)} collective-permute-done((bf16[4096,128]{1,0:T(8,128)(2,1)S(1)}, bf16[4096,128]{1,0:T(8,128)(2,1)S(1)}, u32[]{:S(2)}, u32[]{:S(2)}) %collective-permute-start.12) | collective-permute-done | bytes 1048608 | tf_op jit(solution)/shard_map/ppermute | solution.py:33
  339.5 24.1 %collective-permute-done.13 = bf16[4096,128]{1,0:T(8,128)(2,1)} collective-permute-done((bf16[4096,128]{1,0:T(8,128)(2,1)S(1)}, bf16[4096,128]{1,0:T(8,128)(2,1)}, u32[]{:S(2)}, u32[]{:S(2)}) %collective-permute-start.13) | collective-permute-done | bytes 1048608 | tf_op jit(solution)/shard_map/ppermute | solution.py:33
  364.5 3.8 copy.32
  372.2 7.0 %all-to-all-start.1 = ((bf16[16,2,1024]{2,1,0:T(2,128)(2,1)}), bf16[16,2,1024]{2,1,0:T(2,128)(2,1)S(1)}, u32[]{:S(2)}, u32[]{:S(2)}) async-start(bf16[16,2,1024]{2,1,0:T(2,128)(2,1)} %reshape.124), calls=%async_computation.2 | async-start | bytes 131072 | tf_op jit(solution)/shard_map/all_to_all | solution.py:56
  379.2 2.8 gather_fusion
  382.9 2.9 constant_dynamic-update-slice_fusion.31
  385.8 3.1 constant_dynamic-update-slice_fusion.30
  440.4 6.9 %all-to-all-start = ((bf16[16,2,16,256]{3,2,1,0:T(8,128)(2,1)}), bf16[16,2,16,256]{3,2,1,0:T(8,128)(2,1)S(1)}, u32[]{:S(2)}, u32[]{:S(2)}) async-start(bf16[16,2,16,256]{3,2,1,0:T(8,128)(2,1)} %select_bitcast_fusion), calls=%async_computation.1 | async-start | bytes 524288 | tf_op jit(solution)/shard_map/all_to_all | solution.py:55
  447.3 9.7 %fusion.5 = f32[256,2048]{0,1:T(8,128)} fusion(bf16[256,4096]{1,0:T(8,128)(2,1)S(1)} %bitcast.89, bf16[4096,4096]{1,0:T(8,128)(2,1)} %constant_dynamic-update-slice_fusion, s32[]{:T(128)S(6)} %select_n.38), kind=kOutput, calls=%fused_computation.11 | convolution fusion | flops 4294967296 | bytes 20971524 | tf_op jit(solution)/shard_map/dot_general | solution.py:37
  459.9 3.4 all-reduce
  466.2 6.9 %all-to-all-start.3 = ((bf16[16,2,1024]{2,1,0:T(2,128)(2,1)}), bf16[16,2,1024]{2,1,0:T(2,128)(2,1)S(1)}, u32[]{:S(2)}, u32[]{:S(2)}) async-start(bf16[16,2,1024]{2,1,0:T(2,128)(2,1)} %reshape.128), calls=%async_computation.4 | async-start | bytes 131072 | tf_op jit(solution)/shard_map/all_to_all | solution.py:98
  473.5 3.8 copy.36
  477.3 7.3 %reshape.126 = bf16[16,2,4096]{2,1,0:T(2,128)(2,1)} reshape(bf16[4096,2,16]{2,1,0:T(2,128)(2,1)} %bitcast.91) | data formatting | bytes 524288
  484.6 6.9 %all-to-all-start.2 = ((bf16[16,2,4096]{2,1,0:T(2,128)(2,1)}), bf16[16,2,4096]{2,1,0:T(2,128)(2,1)S(1)}, u32[]{:S(2)}, u32[]{:S(2)}) async-start(bf16[16,2,4096]{2,1,0:T(2,128)(2,1)} %reshape.126), calls=%async_computation.3 | async-start | bytes 524288 | tf_op jit(solution)/shard_map/all_to_all | solution.py:95
  491.5 2.8 fusion.4
  497.2 4.2 all-to-all-done.2
  503.8 4.4 copy.37
  509.6 8.3 %copy.42 = f32[512,256,16]{1,2,0:T(8,128)} copy(f32[512,256,16]{1,0,2:T(8,128)S(1)} %convolution_bitcast_fusion) | data formatting | bytes 16777216
  517.8 8.4 %fusion = f32[4096,256]{0,1:T(8,128)S(1)} fusion(bf16[256,2048]{1,0:T(8,128)(2,1)} %bitcast.98, bf16[4096,4096]{1,0:T(8,128)(2,1)} %constant_dynamic-update-slice_fusion, s32[]{:T(128)S(6)} %select_n.38), kind=kOutput, calls=%fused_computation.2 | convolution fusion | flops 4294967296 | bytes 22020100 | tf_op jit(solution)/shard_map/dot_general | solution.py:39
  (144 shorter events, 86.9 us)
Async XLA Ops:
  7.2 440.2 %copy-start = (bf16[2,128,4096]{2,1,0:T(8,128)(2,1)S(1)}, bf16[2,128,4096]{2,1,0:T(8,128)(2,1)}, u32[]{:S(2)}) copy-start(bf16[2,128,4096]{2,1,0:T(8,128)(2,1)} %param.6) | copy-start | bytes 6291460
  7.2 411.7 %copy-start.2 = (bf16[4096,128]{1,0:T(8,128)(2,1)S(1)}, bf16[4096,128]{1,0:T(8,128)(2,1)}, u32[]{:S(2)}) copy-start(bf16[4096,128]{1,0:T(8,128)(2,1)} %param.7) | copy-start | bytes 3145732
  7.2 30.4 %collective-permute-start = (bf16[4096,128]{1,0:T(8,128)(2,1)}, bf16[4096,128]{1,0:T(8,128)(2,1)S(1)}, u32[]{:S(2)}, u32[]{:S(2)}) collective-permute-start(bf16[4096,128]{1,0:T(8,128)(2,1)} %param.7), channel_id=1, source_target_pairs={{0,2},{2,4},{4,6},{6,8},{8,10},{10,12},{12,14},{14,16},{16,18},{18... | collective-permute-start | bytes 3145736 | tf_op jit(solution)/shard_map/ppermute | solution.py:33
  38.5 27.9 %collective-permute-start.1 = (bf16[4096,128]{1,0:T(8,128)(2,1)S(1)}, bf16[4096,128]{1,0:T(8,128)(2,1)S(1)}, u32[]{:S(2)}, u32[]{:S(2)}) collective-permute-start(bf16[4096,128]{1,0:T(8,128)(2,1)S(1)} %collective-permute-done), channel_id=1, source_target_pairs={{0,2},{2,4},{4,6},{6,8},{8,10},{10,12},{12,14},{14,16},{16,18},{18... | collective-permute-start | bytes 3145736 | tf_op jit(solution)/shard_map/ppermute | solution.py:33
  67.4 27.1 %collective-permute-start.2 = (bf16[4096,128]{1,0:T(8,128)(2,1)S(1)}, bf16[4096,128]{1,0:T(8,128)(2,1)S(1)}, u32[]{:S(2)}, u32[]{:S(2)}) collective-permute-start(bf16[4096,128]{1,0:T(8,128)(2,1)S(1)} %collective-permute-done.1), channel_id=1, source_target_pairs={{0,2},{2,4},{4,6},{6,8},{8,10},{10,12},{12,14},{14,16},{16,18},{18... | collective-permute-start | bytes 3145736 | tf_op jit(solution)/shard_map/ppermute | solution.py:33
  95.5 26.2 %collective-permute-start.3 = (bf16[4096,128]{1,0:T(8,128)(2,1)S(1)}, bf16[4096,128]{1,0:T(8,128)(2,1)S(1)}, u32[]{:S(2)}, u32[]{:S(2)}) collective-permute-start(bf16[4096,128]{1,0:T(8,128)(2,1)S(1)} %collective-permute-done.2), channel_id=1, source_target_pairs={{0,2},{2,4},{4,6},{6,8},{8,10},{10,12},{12,14},{14,16},{16,18},{18... | collective-permute-start | bytes 3145736 | tf_op jit(solution)/shard_map/ppermute | solution.py:33
  122.7 25.4 %collective-permute-start.4 = (bf16[4096,128]{1,0:T(8,128)(2,1)S(1)}, bf16[4096,128]{1,0:T(8,128)(2,1)S(1)}, u32[]{:S(2)}, u32[]{:S(2)}) collective-permute-start(bf16[4096,128]{1,0:T(8,128)(2,1)S(1)} %collective-permute-done.3), channel_id=1, source_target_pairs={{0,2},{2,4},{4,6},{6,8},{8,10},{10,12},{12,14},{14,16},{16,18},{18... | collective-permute-start | bytes 3145736 | tf_op jit(solution)/shard_map/ppermute | solution.py:33
  149.0 24.5 %collective-permute-start.5 = (bf16[4096,128]{1,0:T(8,128)(2,1)S(1)}, bf16[4096,128]{1,0:T(8,128)(2,1)S(1)}, u32[]{:S(2)}, u32[]{:S(2)}) collective-permute-start(bf16[4096,128]{1,0:T(8,128)(2,1)S(1)} %collective-permute-done.4), channel_id=1, source_target_pairs={{0,2},{2,4},{4,6},{6,8},{8,10},{10,12},{12,14},{14,16},{16,18},{18... | collective-permute-start | bytes 3145736 | tf_op jit(solution)/shard_map/ppermute | solution.py:33
  174.5 23.6 %collective-permute-start.6 = (bf16[4096,128]{1,0:T(8,128)(2,1)S(1)}, bf16[4096,128]{1,0:T(8,128)(2,1)S(1)}, u32[]{:S(2)}, u32[]{:S(2)}) collective-permute-start(bf16[4096,128]{1,0:T(8,128)(2,1)S(1)} %collective-permute-done.5), channel_id=1, source_target_pairs={{0,2},{2,4},{4,6},{6,8},{8,10},{10,12},{12,14},{14,16},{16,18},{18... | collective-permute-start | bytes 3145736 | tf_op jit(solution)/shard_map/ppermute | solution.py:33
  199.1 22.8 %collective-permute-start.7 = (bf16[4096,128]{1,0:T(8,128)(2,1)S(1)}, bf16[4096,128]{1,0:T(8,128)(2,1)S(1)}, u32[]{:S(2)}, u32[]{:S(2)}) collective-permute-start(bf16[4096,128]{1,0:T(8,128)(2,1)S(1)} %collective-permute-done.6), channel_id=1, source_target_pairs={{0,2},{2,4},{4,6},{6,8},{8,10},{10,12},{12,14},{14,16},{16,18},{18... | collective-permute-start | bytes 3145736 | tf_op jit(solution)/shard_map/ppermute | solution.py:33
  222.9 22.3 %collective-permute-start.8 = (bf16[4096,128]{1,0:T(8,128)(2,1)S(1)}, bf16[4096,128]{1,0:T(8,128)(2,1)S(1)}, u32[]{:S(2)}, u32[]{:S(2)}) collective-permute-start(bf16[4096,128]{1,0:T(8,128)(2,1)S(1)} %collective-permute-done.7), channel_id=1, source_target_pairs={{0,2},{2,4},{4,6},{6,8},{8,10},{10,12},{12,14},{14,16},{16,18},{18... | collective-permute-start | bytes 3145736 | tf_op jit(solution)/shard_map/ppermute | solution.py:33
  246.2 22.3 %collective-permute-start.9 = (bf16[4096,128]{1,0:T(8,128)(2,1)S(1)}, bf16[4096,128]{1,0:T(8,128)(2,1)S(1)}, u32[]{:S(2)}, u32[]{:S(2)}) collective-permute-start(bf16[4096,128]{1,0:T(8,128)(2,1)S(1)} %collective-permute-done.8), channel_id=1, source_target_pairs={{0,2},{2,4},{4,6},{6,8},{8,10},{10,12},{12,14},{14,16},{16,18},{18... | collective-permute-start | bytes 3145736 | tf_op jit(solution)/shard_map/ppermute | solution.py:33
  269.6 22.3 %collective-permute-start.10 = (bf16[4096,128]{1,0:T(8,128)(2,1)S(1)}, bf16[4096,128]{1,0:T(8,128)(2,1)S(1)}, u32[]{:S(2)}, u32[]{:S(2)}) collective-permute-start(bf16[4096,128]{1,0:T(8,128)(2,1)S(1)} %collective-permute-done.9), channel_id=1, source_target_pairs={{0,2},{2,4},{4,6},{6,8},{8,10},{10,12},{12,14},{14,16},{16,18},{18... | collective-permute-start | bytes 3145736 | tf_op jit(solution)/shard_map/ppermute | solution.py:33
  292.9 22.4 %collective-permute-start.11 = (bf16[4096,128]{1,0:T(8,128)(2,1)S(1)}, bf16[4096,128]{1,0:T(8,128)(2,1)S(1)}, u32[]{:S(2)}, u32[]{:S(2)}) collective-permute-start(bf16[4096,128]{1,0:T(8,128)(2,1)S(1)} %collective-permute-done.10), channel_id=1, source_target_pairs={{0,2},{2,4},{4,6},{6,8},{8,10},{10,12},{12,14},{14,16},{16,18},{18... | collective-permute-start | bytes 3145736 | tf_op jit(solution)/shard_map/ppermute | solution.py:33
  316.2 22.4 %collective-permute-start.12 = (bf16[4096,128]{1,0:T(8,128)(2,1)S(1)}, bf16[4096,128]{1,0:T(8,128)(2,1)S(1)}, u32[]{:S(2)}, u32[]{:S(2)}) collective-permute-start(bf16[4096,128]{1,0:T(8,128)(2,1)S(1)} %collective-permute-done.11), channel_id=1, source_target_pairs={{0,2},{2,4},{4,6},{6,8},{8,10},{10,12},{12,14},{14,16},{16,18},{18... | collective-permute-start | bytes 3145736 | tf_op jit(solution)/shard_map/ppermute | solution.py:33
  339.5 24.1 %collective-permute-start.13 = (bf16[4096,128]{1,0:T(8,128)(2,1)S(1)}, bf16[4096,128]{1,0:T(8,128)(2,1)}, u32[]{:S(2)}, u32[]{:S(2)}) collective-permute-start(bf16[4096,128]{1,0:T(8,128)(2,1)S(1)} %collective-permute-done.12), channel_id=1, source_target_pairs={{0,2},{2,4},{4,6},{6,8},{8,10},{10,12},{12,14},{14,16},{16,18},{18... | collective-permute-start | bytes 3145736 | tf_op jit(solution)/shard_map/ppermute | solution.py:33
  363.7 19.3 %collective-permute-start.14 = (bf16[4096,128]{1,0:T(8,128)(2,1)}, bf16[4096,128]{1,0:T(8,128)(2,1)}, u32[]{:S(2)}, u32[]{:S(2)}) collective-permute-start(bf16[4096,128]{1,0:T(8,128)(2,1)} %collective-permute-done.13), channel_id=1, source_target_pairs={{0,2},{2,4},{4,6},{6,8},{8,10},{10,12},{12,14},{14,16},{16,18},{18... | collective-permute-start | bytes 3145736 | tf_op jit(solution)/shard_map/ppermute | solution.py:33
  372.2 68.2 %all-to-all-start.1 = ((bf16[16,2,1024]{2,1,0:T(2,128)(2,1)}), bf16[16,2,1024]{2,1,0:T(2,128)(2,1)S(1)}, u32[]{:S(2)}, u32[]{:S(2)}) async-start(bf16[16,2,1024]{2,1,0:T(2,128)(2,1)} %reshape.124), calls=%async_computation.2 | async-start | bytes 131072 | tf_op jit(solution)/shard_map/all_to_all | solution.py:56
  382.0 46.0 %copy-start.22 = (bf16[4096,128]{1,0:T(8,128)(2,1)S(1)}, bf16[4096,128]{1,0:T(8,128)(2,1)}, u32[]{:S(2)}) copy-start(bf16[4096,128]{1,0:T(8,128)(2,1)} %copy-done.21) | copy-start | bytes 3145732
  382.0 47.2 %copy-start.20 = (bf16[4096,128]{1,0:T(8,128)(2,1)S(1)}, bf16[4096,128]{1,0:T(8,128)(2,1)}, u32[]{:S(2)}) copy-start(bf16[4096,128]{1,0:T(8,128)(2,1)} %copy-done.19) | copy-start | bytes 3145732
  382.0 48.2 %copy-start.18 = (bf16[4096,128]{1,0:T(8,128)(2,1)S(1)}, bf16[4096,128]{1,0:T(8,128)(2,1)}, u32[]{:S(2)}) copy-start(bf16[4096,128]{1,0:T(8,128)(2,1)} %copy-done.17) | copy-start | bytes 3145732
  382.0 49.3 %copy-start.16 = (bf16[4096,128]{1,0:T(8,128)(2,1)S(1)}, bf16[4096,128]{1,0:T(8,128)(2,1)}, u32[]{:S(2)}) copy-start(bf16[4096,128]{1,0:T(8,128)(2,1)} %copy-done.15) | copy-start | bytes 3145732
  382.1 50.4 %copy-start.14 = (bf16[4096,128]{1,0:T(8,128)(2,1)S(1)}, bf16[4096,128]{1,0:T(8,128)(2,1)}, u32[]{:S(2)}) copy-start(bf16[4096,128]{1,0:T(8,128)(2,1)} %copy-done.13) | copy-start | bytes 3145732
  382.1 51.5 %copy-start.12 = (bf16[4096,128]{1,0:T(8,128)(2,1)S(1)}, bf16[4096,128]{1,0:T(8,128)(2,1)}, u32[]{:S(2)}) copy-start(bf16[4096,128]{1,0:T(8,128)(2,1)} %copy-done.11) | copy-start | bytes 3145732
  382.1 52.6 %copy-start.10 = (bf16[4096,128]{1,0:T(8,128)(2,1)S(1)}, bf16[4096,128]{1,0:T(8,128)(2,1)}, u32[]{:S(2)}) copy-start(bf16[4096,128]{1,0:T(8,128)(2,1)} %copy-done.9) | copy-start | bytes 3145732
  382.1 53.7 %copy-start.8 = (bf16[4096,128]{1,0:T(8,128)(2,1)S(1)}, bf16[4096,128]{1,0:T(8,128)(2,1)}, u32[]{:S(2)}) copy-start(bf16[4096,128]{1,0:T(8,128)(2,1)} %copy-done.7) | copy-start | bytes 3145732
  382.1 54.8 %copy-start.6 = (bf16[4096,128]{1,0:T(8,128)(2,1)S(1)}, bf16[4096,128]{1,0:T(8,128)(2,1)}, u32[]{:S(2)}) copy-start(bf16[4096,128]{1,0:T(8,128)(2,1)} %copy-done.5) | copy-start | bytes 3145732
  382.1 55.9 %copy-start.4 = (bf16[4096,128]{1,0:T(8,128)(2,1)S(1)}, bf16[4096,128]{1,0:T(8,128)(2,1)}, u32[]{:S(2)}) copy-start(bf16[4096,128]{1,0:T(8,128)(2,1)} %copy-done.3) | copy-start | bytes 3145732
  440.4 18.6 %all-to-all-start = ((bf16[16,2,16,256]{3,2,1,0:T(8,128)(2,1)}), bf16[16,2,16,256]{3,2,1,0:T(8,128)(2,1)S(1)}, u32[]{:S(2)}, u32[]{:S(2)}) async-start(bf16[16,2,16,256]{3,2,1,0:T(8,128)(2,1)} %select_bitcast_fusion), calls=%async_computation.1 | async-start | bytes 524288 | tf_op jit(solution)/shard_map/all_to_all | solution.py:55
  447.3 80.9 %reduce-scatter.2.cloned.1.call-start = ((), (), s32[]{:S(2)}) async-start(), calls=%async_computation.5 | async-start | bytes 3145728 | tf_op jit(solution)/shard_map/reduce_scatter | solution.py:38
  466.2 18.5 %all-to-all-start.3 = ((bf16[16,2,1024]{2,1,0:T(2,128)(2,1)}), bf16[16,2,1024]{2,1,0:T(2,128)(2,1)S(1)}, u32[]{:S(2)}, u32[]{:S(2)}) async-start(bf16[16,2,1024]{2,1,0:T(2,128)(2,1)} %reshape.128), calls=%async_computation.4 | async-start | bytes 131072 | tf_op jit(solution)/shard_map/all_to_all | solution.py:98
  484.6 16.8 %all-to-all-start.2 = ((bf16[16,2,4096]{2,1,0:T(2,128)(2,1)}), bf16[16,2,4096]{2,1,0:T(2,128)(2,1)S(1)}, u32[]{:S(2)}, u32[]{:S(2)}) async-start(bf16[16,2,4096]{2,1,0:T(2,128)(2,1)} %reshape.126), calls=%async_computation.3 | async-start | bytes 524288 | tf_op jit(solution)/shard_map/all_to_all | solution.py:95
  (18 other events, 192.4 us)
Sparse Core Ops, SparseCore 0:
  457.2 11.0 reduce-scatter.1
